TPU v7x, 32 devices: a whole 2x2x4 slice. The times are simulated.
32 devices in a mesh: wide: 8 (over z, x), narrow: 4 (over y, core).
Axes of the slice: x: 2, y: 2, z: 4, core: 2. Of those that a mesh axis runs over, the one named last changes fastest.
Arguments:
- pressure: float32 [1024, 128], P(('wide', 'narrow')), may hold values from -6 to 6
- right_side: float32 [1024, 128], P(('wide', 'narrow')), may hold values from -6 to 6
- concentration: float32 [1024, 128], P(('wide', 'narrow')), may hold values from 0 to 1
- pore_volume: float32 [1024, 128], P(('wide', 'narrow')), may hold values from 0.5 to 2
- well_rate: float32 [1024, 128], P(('wide', 'narrow')), may hold values from 0.02 to 0.5
- inject_conc: float32 [1024, 128], P(('wide', 'narrow')), may hold values from 0 to 1
- transmissibility: float32 [6, 131072], P(None, ('wide', 'narrow')), may hold values from 0.1 to 1
- face_neighbor: int32 [6, 1024], P(None, ('wide', 'narrow')), may hold values from 0 to 56, as said below
- sub_matrix: bfloat16 [2048, 4, 128, 128], P(('wide', 'narrow')), as said below
- sub_columns: int32 [2048, 4], P(('wide', 'narrow')), may hold values from 0 to 63, as said below
- send_blocks: int32 [32, 4, 8], P(('wide', 'narrow')), may hold values from 0 to 31, as said below
- send_counts: int32 [32, 4], P(('wide', 'narrow')), may hold values from 1 to 8, as said below
- basis_weights: bfloat16 [8192, 4096], P(('wide', 'narrow')), may hold values from -0.09375 to 0.09375
- coarse_index: int32 [8192], P(('wide', 'narrow')), may hold values from 0 to 4095, as said below
- coarse_inverse: float32 [4096, 512], P(('wide', 'narrow')), may hold values from -0.25 to 0.25
Outputs:
- pressure_new: float32 [1024, 128], P(('wide', 'narrow'))
- concentration_new: float32 [1024, 128], P(('wide', 'narrow'))
Inputs may be any that keep to these rules, and one draw needn't show every extreme that they name: `send_blocks`: local block indices below 32. `send_counts`: between 1 and 8; the first subdomain sends 8 blocks to every neighbour and the last sends one. `sub_columns`: slot 0 of each row block names the row block itself. `face_neighbor`: each owned block's faces name owned blocks or the first received block from some neighbour. `coarse_index`: a subdomain's functions may be owned by any index of wide, and may repeat. `sub_matrix`: the diagonal of each row block's first stored block lies between 0.9 and 2.1.
All inputs are finite; a program needn't handle non-finite values.
Results may differ from a plain program's by a relative error of at most 0.00225.
The roundings to bfloat16 on the way count: a program that leaves them out, or rounds other values in their place, can miss the bound.
Values may be sent and summed in bfloat16 or wider, within the bound.
A program may use at most 64 MiB of HBM per device.

v0:
```python
import jax
import jax.numpy as jnp
from jax import lax
from jax.sharding import PartitionSpec as P

SWEEPS = 4
shift_offsets = (2, 1, -1, -2)
courant = 0.9


def from_behind(value, axis, steps):
    count = lax.axis_size(axis)
    leading, last = (max(0, -steps), min(count, count - steps))
    return lax.ppermute(value, axis, [(source, source + steps) for source in range(leading, last)])


def block_product(matrix, columns, vector_b):
    picked = vector_b[columns]
    return jnp.einsum("rkij,rkj->ri", matrix, picked, preferred_element_type=jnp.float32)


def outgoing_one(owned_rows, send_blocks, send_counts):
    slot_count = send_blocks.shape[-1]
    active = jnp.arange(slot_count)[None, :] < send_counts[0][:, None]
    picked = owned_rows[send_blocks[0]]
    return jnp.where(active[:, :, None], picked, jnp.zeros_like(picked))


def with_rims(owned_list, send_blocks, send_counts, mover):
    packed = [outgoing_one(owned_rows, send_blocks, send_counts) for owned_rows in owned_list]
    arrived = [[owned_rows] for owned_rows in owned_list]
    for position, offset in enumerate(shift_offsets):
        moved_rows = mover([sent_rows[position] for sent_rows in packed], offset)
        for target, portion in zip(arrived, moved_rows):
            target.append(portion)
    return [jnp.concatenate(target, axis=0) for target in arrived]


def local(
    pressure,
    right_side,
    concentration,
    pore_volume,
    well_rate,
    inject_conc,
    transmissibility,
    face_neighbor,
    sub_matrix,
    sub_columns,
    send_blocks,
    send_counts,
    basis_weights,
    coarse_index,
    coarse_inverse,
):
    owned_count = pressure.shape[0]
    pressure_b = pressure.astype(jnp.bfloat16)
    ext_pressure = with_rims(
        [pressure_b],
        send_blocks,
        send_counts,
        lambda members, offset: (from_behind(members[0], "wide", offset),),
    )[0]
    residual = right_side - block_product(
        sub_matrix[:owned_count], sub_columns[:owned_count], ext_pressure
    )
    residual_b = residual.astype(jnp.bfloat16)
    local_coarse = jnp.dot(
        basis_weights, residual_b.reshape(-1), preferred_element_type=jnp.float32
    )
    coarse_width = coarse_inverse.shape[1]
    wide_count = lax.axis_size("wide")
    coarse_total = coarse_width * wide_count
    ext_residual = with_rims(
        [residual_b],
        send_blocks,
        send_counts,
        lambda members, offset: (from_behind(members[0], "wide", offset),),
    )[0]
    diagonal = jnp.diagonal(sub_matrix[:, 0], axis1=1, axis2=2).astype(jnp.float32)
    target_rows = ext_residual.astype(jnp.float32)
    update = jnp.zeros(target_rows.shape, jnp.float32)
    for turn_index in range(SWEEPS):
        update = (
            update
            + (target_rows - block_product(sub_matrix, sub_columns, update.astype(jnp.bfloat16)))
            / diagonal
        )
    partial_value = jnp.zeros((coarse_total,), jnp.float32).at[coarse_index].add(local_coarse)
    summed = lax.psum(partial_value, ("wide", "narrow"))
    owner_block = lax.dynamic_slice_in_dim(
        summed, lax.axis_index("wide") * coarse_width, coarse_width
    )
    block_inverse = lax.all_gather(coarse_inverse, "narrow", axis=0, tiled=True)
    owner_values = jnp.dot(block_inverse, owner_block, precision=lax.Precision.HIGHEST)
    coarse_values = lax.all_gather(owner_values, "wide", axis=0, tiled=True)
    picked_coarse = coarse_values.astype(jnp.bfloat16)[coarse_index]
    correction = jnp.dot(picked_coarse, basis_weights, preferred_element_type=jnp.float32)
    pressure_next = pressure + update[:owned_count] + correction.reshape(owned_count, -1)
    ext_next, ext_conc = with_rims(
        [pressure_next, concentration],
        send_blocks,
        send_counts,
        lambda members, offset: from_behind((members[0], members[1]), "wide", offset),
    )
    face_count = face_neighbor.shape[0]
    near_pressure = ext_next[face_neighbor].reshape(face_count, -1)
    near_conc = ext_conc[face_neighbor].reshape(face_count, -1)
    own_pressure = pressure_next.reshape(1, -1)
    conc_flat = concentration.reshape(-1)
    face_flux = transmissibility * (own_pressure - near_pressure)
    outward = jnp.maximum(face_flux, 0.0)
    inward = jnp.minimum(face_flux, 0.0)
    advection = jnp.sum(outward * conc_flat[None, :] + inward * near_conc, axis=0)
    outflow = jnp.sum(outward, axis=0)
    volume_flat = pore_volume.reshape(-1)
    rate_flat = well_rate.reshape(-1)
    cell_rate = (outflow + rate_flat) / volume_flat
    rate_top = lax.pmax(jnp.max(cell_rate), ("wide", "narrow"))
    time_step = courant / rate_top
    conc_next = conc_flat + time_step / volume_flat * (
        rate_flat * (inject_conc.reshape(-1) - conc_flat) - advection
    )
    return (pressure_next, conc_next.reshape(owned_count, -1))


def solution(mesh):
    return jax.shard_map(
        local,
        mesh=mesh,
        in_specs=(
            P(("wide", "narrow"), None),
            P(("wide", "narrow"), None),
            P(("wide", "narrow"), None),
            P(("wide", "narrow"), None),
            P(("wide", "narrow"), None),
            P(("wide", "narrow"), None),
            P(None, ("wide", "narrow")),
            P(None, ("wide", "narrow")),
            P(("wide", "narrow"), None, None, None),
            P(("wide", "narrow"), None),
            P(("wide", "narrow"), None, None),
            P(("wide", "narrow"), None),
            P(("wide", "narrow"), None),
            P(("wide", "narrow")),
            P(("wide", "narrow"), None),
        ),
        out_specs=(P(("wide", "narrow"), None), P(("wide", "narrow"), None)),
        check_vma=False,
    )
```

profile of v0, /device:TPU:0, one launch (start us, length us, event | category | flops | bytes accessed | tf_op | source)
XLA Modules:
  0.0 232.3 jit_solution(17184199817668447989)
XLA Ops:
  10.3 4.9 %collective-permute-start = (bf16[8,128]{1,0:T(8,128)(2,1)S(1)}, bf16[8,128]{1,0:T(8,128)(2,1)S(1)}, u32[]{:S(2)}, u32[]{:S(2)}) collective-permute-start(bf16[8,128]{1,0:T(8,128)(2,1)S(1)} %get-tuple-element.29), channel_id=1, source_target_pairs={{0,8},{4,12},{8,16},{12,20},{16,24},{20,28},{1,9},{5,13},{9,17},{1... | collective-permute-start | bytes 6152 | tf_op jit(solution)/shard_map/ppermute | solution.py:14
  15.2 3.4 %collective-permute-start.1 = (bf16[8,128]{1,0:T(8,128)(2,1)S(1)}, bf16[8,128]{1,0:T(8,128)(2,1)S(1)}, u32[]{:S(2)}, u32[]{:S(2)}) collective-permute-start(bf16[8,128]{1,0:T(8,128)(2,1)S(1)} %get-tuple-element.28), channel_id=1, source_target_pairs={{0,4},{4,8},{8,12},{12,16},{16,20},{20,24},{24,28},{1,5},{5,9},{9,... | collective-permute-start | bytes 6152 | tf_op jit(solution)/shard_map/ppermute | solution.py:14
  23.5 3.2 %slice.70 = bf16[64,1,128,128]{3,2,1,0:T(8,128)(2,1)} slice(bf16[64,4,128,128]{3,2,1,0:T(8,128)(2,1)} %param.23), slice={[0:64], [0:1], [0:128], [0:128]} | slice | bytes 4194304 | tf_op jit(solution)/shard_map/slice | solution.py:80
  26.7 5.3 %copy.38 = bf16[64,1,128,128]{0,3,2,1:T(8,128)(2,1)} copy(bf16[64,1,128,128]{3,2,1,0:T(8,128)(2,1)} %slice.70) | data formatting | bytes 4194304
  32.1 1.9 gather_fusion.4
  35.2 5.7 %fusion.8 = f32[64,1,128,1]{2,1,3,0:T(1,128)S(1)} fusion(bf16[64,4,128,128]{3,2,1,0:T(8,128)(2,1)} %param.23, bf16[64,4,128,1]{2,1,0,3:T(4,128)(2,1)S(1)} %bitcast.134), kind=kOutput, calls=%fused_computation.23 | convolution fusion | flops 8388608 | bytes 8486912 | tf_op jit(solution)/shard_map/rkij,rkj->ri/dot_general | solution.py:19
  42.4 3.4 %fusion = f32[32,1,128,1]{2,1,3,0:T(1,128)S(1)} fusion(bf16[64,4,128,128]{3,2,1,0:T(8,128)(2,1)} %param.23, bf16[32,4,128,1]{2,1,0,3:T(4,128)(2,1)S(1)} %bitcast.143), kind=kOutput, calls=%fused_computation.14 | convolution fusion | flops 4194304 | bytes 4243456 | tf_op jit(solution)/shard_map/rkij,rkj->ri/dot_general | solution.py:19
  46.5 6.3 %collective-permute-start.4 = (bf16[8,128]{1,0:T(8,128)(2,1)S(1)}, bf16[8,128]{1,0:T(8,128)(2,1)S(1)}, u32[]{:S(2)}, u32[]{:S(2)}) collective-permute-start(bf16[8,128]{1,0:T(8,128)(2,1)S(1)} %get-tuple-element.25), channel_id=1, source_target_pairs={{0,8},{4,12},{8,16},{12,20},{16,24},{20,28},{1,9},{5,13},{9,17},{1... | collective-permute-start | bytes 6152 | tf_op jit(solution)/shard_map/ppermute | solution.py:14
  53.5 2.0 scatter_custom_fusion
  55.4 40.0 %psum.7 = f32[4096]{0:T(1024)S(1)} all-reduce(f32[4096]{0:T(1024)S(1)} %scatter_custom_fusion), channel_id=1, replica_groups=mesh['wide'=8,'narrow'=4] {'wide','narrow'}, use_global_device_ids=true, to_apply=%region_1.2 | all-reduce | flops 4096 | bytes 32768 | tf_op jit(solution)/shard_map/psum | solution.py:90
  95.4 4.2 %collective-permute-start.5 = (bf16[8,128]{1,0:T(8,128)(2,1)S(1)}, bf16[8,128]{1,0:T(8,128)(2,1)S(1)}, u32[]{:S(2)}, u32[]{:S(2)}) collective-permute-start(bf16[8,128]{1,0:T(8,128)(2,1)S(1)} %get-tuple-element.24), channel_id=1, source_target_pairs={{0,4},{4,8},{8,12},{12,16},{16,20},{20,24},{24,28},{1,5},{5,9},{9,... | collective-permute-start | bytes 6152 | tf_op jit(solution)/shard_map/ppermute | solution.py:14
  102.5 2.6 %collective-permute-done.6 = bf16[8,128]{1,0:T(8,128)(2,1)S(1)} collective-permute-done((bf16[8,128]{1,0:T(8,128)(2,1)S(1)}, bf16[8,128]{1,0:T(8,128)(2,1)S(1)}, u32[]{:S(2)}, u32[]{:S(2)}) %collective-permute-start.6) | collective-permute-done | bytes 2080 | tf_op jit(solution)/shard_map/ppermute | solution.py:14
  107.4 5.6 %fusion.6 = f32[64,1,128,1]{2,1,3,0:T(1,128)S(1)} fusion(bf16[64,4,128,128]{3,2,1,0:T(8,128)(2,1)} %param.23, bf16[64,4,128,1]{2,1,0,3:T(4,128)(2,1)S(1)} %bitcast.135), kind=kOutput, calls=%fused_computation.21 | convolution fusion | flops 8388608 | bytes 8486912 | tf_op jit(solution)/shard_map/rkij,rkj->ri/dot_general | solution.py:19
  113.9 5.6 %fusion.4 = f32[64,1,128,1]{2,1,3,0:T(1,128)S(1)} fusion(bf16[64,4,128,128]{3,2,1,0:T(8,128)(2,1)} %param.23, bf16[64,4,128,1]{2,1,0,3:T(4,128)(2,1)S(1)} %bitcast.136), kind=kOutput, calls=%fused_computation.19 | convolution fusion | flops 8388608 | bytes 8486912 | tf_op jit(solution)/shard_map/rkij,rkj->ri/dot_general | solution.py:19
  120.5 5.6 %fusion.2 = f32[64,1,128,1]{2,1,3,0:T(1,128)S(1)} fusion(bf16[64,4,128,128]{3,2,1,0:T(8,128)(2,1)} %param.23, bf16[64,4,128,1]{2,1,0,3:T(4,128)(2,1)S(1)} %bitcast.133), kind=kOutput, calls=%fused_computation.17 | convolution fusion | flops 8388608 | bytes 8486912 | tf_op jit(solution)/shard_map/rkij,rkj->ri/dot_general | solution.py:19
  126.1 2.2 convolution_bitcast_fusion
  128.3 26.0 %all-gather = bf16[8,1,512]{2,1,0:T(2,128)(2,1)S(1)} all-gather(bf16[1,1,512]{2,1,0:T(2,128)(2,1)S(1)} %convolution_bitcast_fusion), channel_id=1, replica_groups=mesh['wide'=8,'narrow'=4] {'wide'}, dimensions={0}, use_global_device_ids=true | all-gather | bytes 9216 | tf_op jit(solution)/shard_map/all_gather | solution.py:96
  154.4 1.9 gather_fusion.8
  157.4 2.1 collective-permute-start.8
  163.9 6.5 %collective-permute-start.12 = (f32[8,128]{1,0:T(8,128)S(1)}, f32[8,128]{1,0:T(8,128)S(1)}, u32[]{:S(2)}, u32[]{:S(2)}) collective-permute-start(f32[8,128]{1,0:T(8,128)S(1)} %get-tuple-element.17), channel_id=1, source_target_pairs={{0,8},{4,12},{8,16},{12,20},{16,24},{20,28},{1,9},{5,13},{9,17},{1... | collective-permute-start | bytes 12296 | tf_op jit(solution)/shard_map/ppermute | solution.py:14
  170.4 2.6 %collective-permute-start.13 = (f32[8,128]{1,0:T(8,128)S(1)}, f32[8,128]{1,0:T(8,128)S(1)}, u32[]{:S(2)}, u32[]{:S(2)}) collective-permute-start(f32[8,128]{1,0:T(8,128)S(1)} %get-tuple-element.16), channel_id=1, source_target_pairs={{0,4},{4,8},{8,12},{12,16},{16,20},{20,24},{24,28},{1,5},{5,9},{9,... | collective-permute-start | bytes 12296 | tf_op jit(solution)/shard_map/ppermute | solution.py:14
  175.8 3.5 %collective-permute-done.14 = f32[8,128]{1,0:T(8,128)S(1)} collective-permute-done((f32[8,128]{1,0:T(8,128)S(1)}, f32[8,128]{1,0:T(8,128)S(1)}, u32[]{:S(2)}, u32[]{:S(2)}) %collective-permute-start.14) | collective-permute-done | bytes 4128 | tf_op jit(solution)/shard_map/ppermute | solution.py:14
  180.0 2.7 %collective-permute-done.15 = f32[8,128]{1,0:T(8,128)S(1)} collective-permute-done((f32[8,128]{1,0:T(8,128)S(1)}, f32[8,128]{1,0:T(8,128)S(1)}, u32[]{:S(2)}, u32[]{:S(2)}) %collective-permute-start.15) | collective-permute-done | bytes 4128 | tf_op jit(solution)/shard_map/ppermute | solution.py:14
  184.2 39.9 %pmax.7 = f32[]{:T(128)} all-reduce(f32[]{:T(128)} %fusion.16), channel_id=1, replica_groups=mesh['wide'=8,'narrow'=4] {'wide','narrow'}, use_global_device_ids=true, to_apply=%region_4.5 | all-reduce | flops 1 | bytes 8 | tf_op jit(solution)/shard_map/pmax | solution.py:119
  (120 shorter events, 29.7 us)
Async XLA Ops:
  7.2 45.6 %copy-start = (bf16[256,4096]{1,0:T(8,128)(2,1)S(1)}, bf16[256,4096]{1,0:T(8,128)(2,1)}, u32[]{:S(2)}) copy-start(bf16[256,4096]{1,0:T(8,128)(2,1)} %param.27) | copy-start | bytes 6291460
  7.2 118.9 %all-gather.3.cloned.1.call-start = ((), (), s32[]{:S(2)}) async-start(), calls=%async_computation | async-start | bytes 1310720 | tf_op jit(solution)/shard_map/all_gather | solution.py:94
  10.3 31.3 %collective-permute-start = (bf16[8,128]{1,0:T(8,128)(2,1)S(1)}, bf16[8,128]{1,0:T(8,128)(2,1)S(1)}, u32[]{:S(2)}, u32[]{:S(2)}) collective-permute-start(bf16[8,128]{1,0:T(8,128)(2,1)S(1)} %get-tuple-element.29), channel_id=1, source_target_pairs={{0,8},{4,12},{8,16},{12,20},{16,24},{20,28},{1,9},{5,13},{9,17},{1... | collective-permute-start | bytes 6152 | tf_op jit(solution)/shard_map/ppermute | solution.py:14
  15.2 26.4 %collective-permute-start.1 = (bf16[8,128]{1,0:T(8,128)(2,1)S(1)}, bf16[8,128]{1,0:T(8,128)(2,1)S(1)}, u32[]{:S(2)}, u32[]{:S(2)}) collective-permute-start(bf16[8,128]{1,0:T(8,128)(2,1)S(1)} %get-tuple-element.28), channel_id=1, source_target_pairs={{0,4},{4,8},{8,12},{12,16},{16,20},{20,24},{24,28},{1,5},{5,9},{9,... | collective-permute-start | bytes 6152 | tf_op jit(solution)/shard_map/ppermute | solution.py:14
  18.6 23.0 %collective-permute-start.2 = (bf16[8,128]{1,0:T(8,128)(2,1)S(1)}, bf16[8,128]{1,0:T(8,128)(2,1)S(1)}, u32[]{:S(2)}, u32[]{:S(2)}) collective-permute-start(bf16[8,128]{1,0:T(8,128)(2,1)S(1)} %get-tuple-element.27), channel_id=1, source_target_pairs={{4,0},{8,4},{12,8},{16,12},{20,16},{24,20},{28,24},{5,1},{9,5},{13... | collective-permute-start | bytes 6152 | tf_op jit(solution)/shard_map/ppermute | solution.py:14
  19.9 21.8 %collective-permute-start.3 = (bf16[8,128]{1,0:T(8,128)(2,1)S(1)}, bf16[8,128]{1,0:T(8,128)(2,1)S(1)}, u32[]{:S(2)}, u32[]{:S(2)}) collective-permute-start(bf16[8,128]{1,0:T(8,128)(2,1)S(1)} %get-tuple-element.26), channel_id=1, source_target_pairs={{8,0},{12,4},{16,8},{20,12},{24,16},{28,20},{9,1},{13,5},{17,9},{2... | collective-permute-start | bytes 6152 | tf_op jit(solution)/shard_map/ppermute | solution.py:14
  46.5 56.0 %collective-permute-start.4 = (bf16[8,128]{1,0:T(8,128)(2,1)S(1)}, bf16[8,128]{1,0:T(8,128)(2,1)S(1)}, u32[]{:S(2)}, u32[]{:S(2)}) collective-permute-start(bf16[8,128]{1,0:T(8,128)(2,1)S(1)} %get-tuple-element.25), channel_id=1, source_target_pairs={{0,8},{4,12},{8,16},{12,20},{16,24},{20,28},{1,9},{5,13},{9,17},{1... | collective-permute-start | bytes 6152 | tf_op jit(solution)/shard_map/ppermute | solution.py:14
  95.4 7.1 %collective-permute-start.5 = (bf16[8,128]{1,0:T(8,128)(2,1)S(1)}, bf16[8,128]{1,0:T(8,128)(2,1)S(1)}, u32[]{:S(2)}, u32[]{:S(2)}) collective-permute-start(bf16[8,128]{1,0:T(8,128)(2,1)S(1)} %get-tuple-element.24), channel_id=1, source_target_pairs={{0,4},{4,8},{8,12},{12,16},{16,20},{20,24},{24,28},{1,5},{5,9},{9,... | collective-permute-start | bytes 6152 | tf_op jit(solution)/shard_map/ppermute | solution.py:14
  99.6 5.5 %collective-permute-start.6 = (bf16[8,128]{1,0:T(8,128)(2,1)S(1)}, bf16[8,128]{1,0:T(8,128)(2,1)S(1)}, u32[]{:S(2)}, u32[]{:S(2)}) collective-permute-start(bf16[8,128]{1,0:T(8,128)(2,1)S(1)} %get-tuple-element.23), channel_id=1, source_target_pairs={{4,0},{8,4},{12,8},{16,12},{20,16},{24,20},{28,24},{5,1},{9,5},{13... | collective-permute-start | bytes 6152 | tf_op jit(solution)/shard_map/ppermute | solution.py:14
  100.9 5.6 %collective-permute-start.7 = (bf16[8,128]{1,0:T(8,128)(2,1)S(1)}, bf16[8,128]{1,0:T(8,128)(2,1)S(1)}, u32[]{:S(2)}, u32[]{:S(2)}) collective-permute-start(bf16[8,128]{1,0:T(8,128)(2,1)S(1)} %get-tuple-element.22), channel_id=1, source_target_pairs={{8,0},{12,4},{16,8},{20,12},{24,16},{28,20},{9,1},{13,5},{17,9},{2... | collective-permute-start | bytes 6152 | tf_op jit(solution)/shard_map/ppermute | solution.py:14
  119.5 37.2 %copy-start.6 = (f32[32,128]{1,0:T(8,128)S(1)}, f32[32,128]{1,0:T(8,128)}, u32[]{:S(2)}) copy-start(f32[32,128]{1,0:T(8,128)} %param.15) | copy-start | bytes 49156
  119.5 63.9 %copy-start.3 = (f32[6,4096]{1,0:T(8,128)S(1)}, f32[6,4096]{1,0:T(8,128)}, u32[]{:S(2)}) copy-start(f32[6,4096]{1,0:T(8,128)} %param.21) | copy-start | bytes 294916
  119.5 64.0 %copy-start.4 = (f32[32,128]{1,0:T(8,128)S(1)}, f32[32,128]{1,0:T(8,128)}, u32[]{:S(2)}) copy-start(f32[32,128]{1,0:T(8,128)} %param.19) | copy-start | bytes 49156
  119.5 64.0 %copy-start.5 = (f32[32,128]{1,0:T(8,128)S(1)}, f32[32,128]{1,0:T(8,128)}, u32[]{:S(2)}) copy-start(f32[32,128]{1,0:T(8,128)} %param.18) | copy-start | bytes 49156
  119.6 105.2 %copy-start.8 = (f32[32,128]{1,0:T(8,128)S(1)}, f32[32,128]{1,0:T(8,128)}, u32[]{:S(2)}) copy-start(f32[32,128]{1,0:T(8,128)} %param.20) | copy-start | bytes 49156
  156.7 68.7 %copy-start.2 = (f32[32,128]{1,0:T(8,128)}, f32[32,128]{1,0:T(8,128)S(1)}, u32[]{:S(2)}) copy-start(f32[32,128]{1,0:T(8,128)S(1)} %get-tuple-element.5) | copy-start | bytes 49156
  157.4 13.0 %collective-permute-start.8 = (f32[8,128]{1,0:T(8,128)S(1)}, f32[8,128]{1,0:T(8,128)S(1)}, u32[]{:S(2)}, u32[]{:S(2)}) collective-permute-start(f32[8,128]{1,0:T(8,128)S(1)} %get-tuple-element.21), channel_id=1, source_target_pairs={{0,8},{4,12},{8,16},{12,20},{16,24},{20,28},{1,9},{5,13},{9,17},{1... | collective-permute-start | bytes 12296 | tf_op jit(solution)/shard_map/ppermute | solution.py:14
  159.5 13.5 %collective-permute-start.9 = (f32[8,128]{1,0:T(8,128)S(1)}, f32[8,128]{1,0:T(8,128)S(1)}, u32[]{:S(2)}, u32[]{:S(2)}) collective-permute-start(f32[8,128]{1,0:T(8,128)S(1)} %get-tuple-element.20), channel_id=1, source_target_pairs={{0,4},{4,8},{8,12},{12,16},{16,20},{20,24},{24,28},{1,5},{5,9},{9,... | collective-permute-start | bytes 12296 | tf_op jit(solution)/shard_map/ppermute | solution.py:14
  161.3 13.1 %collective-permute-start.10 = (f32[8,128]{1,0:T(8,128)S(1)}, f32[8,128]{1,0:T(8,128)S(1)}, u32[]{:S(2)}, u32[]{:S(2)}) collective-permute-start(f32[8,128]{1,0:T(8,128)S(1)} %get-tuple-element.19), channel_id=1, source_target_pairs={{4,0},{8,4},{12,8},{16,12},{20,16},{24,20},{28,24},{5,1},{9,5},{13... | collective-permute-start | bytes 12296 | tf_op jit(solution)/shard_map/ppermute | solution.py:14
  162.6 13.1 %collective-permute-start.11 = (f32[8,128]{1,0:T(8,128)S(1)}, f32[8,128]{1,0:T(8,128)S(1)}, u32[]{:S(2)}, u32[]{:S(2)}) collective-permute-start(f32[8,128]{1,0:T(8,128)S(1)} %get-tuple-element.18), channel_id=1, source_target_pairs={{8,0},{12,4},{16,8},{20,12},{24,16},{28,20},{9,1},{13,5},{17,9},{2... | collective-permute-start | bytes 12296 | tf_op jit(solution)/shard_map/ppermute | solution.py:14
  163.9 11.8 %collective-permute-start.12 = (f32[8,128]{1,0:T(8,128)S(1)}, f32[8,128]{1,0:T(8,128)S(1)}, u32[]{:S(2)}, u32[]{:S(2)}) collective-permute-start(f32[8,128]{1,0:T(8,128)S(1)} %get-tuple-element.17), channel_id=1, source_target_pairs={{0,8},{4,12},{8,16},{12,20},{16,24},{20,28},{1,9},{5,13},{9,17},{1... | collective-permute-start | bytes 12296 | tf_op jit(solution)/shard_map/ppermute | solution.py:14
  170.4 5.3 %collective-permute-start.13 = (f32[8,128]{1,0:T(8,128)S(1)}, f32[8,128]{1,0:T(8,128)S(1)}, u32[]{:S(2)}, u32[]{:S(2)}) collective-permute-start(f32[8,128]{1,0:T(8,128)S(1)} %get-tuple-element.16), channel_id=1, source_target_pairs={{0,4},{4,8},{8,12},{12,16},{16,20},{20,24},{24,28},{1,5},{5,9},{9,... | collective-permute-start | bytes 12296 | tf_op jit(solution)/shard_map/ppermute | solution.py:14
  173.1 6.2 %collective-permute-start.14 = (f32[8,128]{1,0:T(8,128)S(1)}, f32[8,128]{1,0:T(8,128)S(1)}, u32[]{:S(2)}, u32[]{:S(2)}) collective-permute-start(f32[8,128]{1,0:T(8,128)S(1)} %get-tuple-element.15), channel_id=1, source_target_pairs={{4,0},{8,4},{12,8},{16,12},{20,16},{24,20},{28,24},{5,1},{9,5},{13... | collective-permute-start | bytes 12296 | tf_op jit(solution)/shard_map/ppermute | solution.py:14
  174.4 8.3 %collective-permute-start.15 = (f32[8,128]{1,0:T(8,128)S(1)}, f32[8,128]{1,0:T(8,128)S(1)}, u32[]{:S(2)}, u32[]{:S(2)}) collective-permute-start(f32[8,128]{1,0:T(8,128)S(1)} %get-tuple-element.14), channel_id=1, source_target_pairs={{8,0},{12,4},{16,8},{20,12},{24,16},{28,20},{9,1},{13,5},{17,9},{2... | collective-permute-start | bytes 12296 | tf_op jit(solution)/shard_map/ppermute | solution.py:14
  (3 other events, 42.1 us)
Sparse Core Ops, SparseCore 0:
  21.3 20.1 all-gather.2
where the time goes:
time: 233 us; the launch traced here: 232 us
  blocking collectives  106 us (45%)
  starting transfers between devices  42.4 us (18%)
  matrix products  29.2 us (13%)
  local copies, waits for them, and re-layouts  21.3 us (9%)
  between operations  15.3 us (7%)
  waiting for transfers between devices  10.2 us (4%)
  other arithmetic  8.01 us (3%)
    ppermute x16, starting transfers between devices, from_behind(): lax.ppermute(value, axis, [(source, source + steps) for source in range(l...  42.3 us
    psum x1, blocking collectives, local(): summed = lax.psum(partial_value, ('wide', 'narrow'))  40 us
    pmax x1, blocking collectives, local(): rate_top = lax.pmax(jnp.max(cell_rate), ('wide', 'narrow'))  39.9 us
    all_gather x1, blocking collectives, local(): coarse_values = lax.all_gather(owner_values, 'wide', axis=0, tiled=True)  26 us
    dot_general x5, matrix products, block_product(): jnp.einsum('rkij,rkj->ri', matrix, picked, preferred_element_type=jnp.flo...  26 us
    ppermute x16, waiting for transfers between devices, from_behind(): lax.ppermute(value, axis, [(source, source + steps) for source in range(l...  10.2 us
    unnamed x35, local copies, waits for them, and re-layouts  5.47 us
  transfers between devices with their start and end apart: 17, of which 4 were waited for; matrix products, arithmetic and copies ran while one was open for 21% of the time, Pallas kernels for 0%

commit v1 on v0

--- a/solution.py
+++ b/solution.py
@@ -6,6 +6,20 @@
 SWEEPS = 4
 shift_offsets = (2, 1, -1, -2)
 courant = 0.9
+
+
+def _spread_frame(patch, group_axis, where_dim):
+    sides = jax.lax.axis_size(group_axis)
+    oldest = patch
+    buffer = [oldest]
+    passed = list(map(lambda tick: (tick - 1, tick), range(1, sides))) + [(sides - 1, 0)]
+    for _ in range(sides - 1):
+        oldest = jax.lax.ppermute(oldest, group_axis, passed)
+        buffer += [oldest]
+    known = jnp.concatenate([*reversed(buffer)], axis=where_dim)
+    return jnp.roll(
+        known, shift=(jax.lax.axis_index(group_axis) + 1) * oldest.shape[where_dim], axis=where_dim
+    )
 
 
 def from_behind(value, axis, steps):
@@ -93,7 +107,7 @@
     )
     block_inverse = lax.all_gather(coarse_inverse, "narrow", axis=0, tiled=True)
     owner_values = jnp.dot(block_inverse, owner_block, precision=lax.Precision.HIGHEST)
-    coarse_values = lax.all_gather(owner_values, "wide", axis=0, tiled=True)
+    coarse_values = _spread_frame(owner_values, "wide", 0)
     picked_coarse = coarse_values.astype(jnp.bfloat16)[coarse_index]
     correction = jnp.dot(picked_coarse, basis_weights, preferred_element_type=jnp.float32)
     pressure_next = pressure + update[:owned_count] + correction.reshape(owned_count, -1)

time: 233 us -> 232 us (level)
  blocking collectives: 106 us -> 81.1 us
  waiting for transfers between devices: 10.2 us -> 32.8 us
    all_gather x1 -> x0, blocking collectives: 26 us -> none  [local(): coarse_values = lax.all_gather(owner_values, 'wide', axis=0, tiled=True)]
    ppermute x0 -> x7, waiting for transfers between devices: none -> 23.4 us  [_spread_frame(): oldest = jax.lax.ppermute(oldest, group_axis, passed)]
    unnamed x35 -> x49, local copies, waits for them, and re-layouts: 5.47 us -> 5.52 us
  transfers between devices with their start and end apart: 17 -> 24, of which waited for: 4 -> 10; matrix products, arithmetic and copies ran while one was open for 21% -> 22% of each run, Pallas kernels for 0% -> 0%
where the time goes in v1:
time: 232 us; the launch traced here: 231 us
  blocking collectives  81.1 us (35%)
  starting transfers between devices  43.2 us (19%)
  waiting for transfers between devices  32.8 us (14%)
  matrix products  29.2 us (13%)
  local copies, waits for them, and re-layouts  21.4 us (9%)
  between operations  15.4 us (7%)
  other arithmetic  8 us (3%)
    ppermute x16, starting transfers between devices, from_behind(): lax.ppermute(value, axis, [(source, source + steps) for source in range(l...  42.2 us
    pmax x1, blocking collectives, local(): rate_top = lax.pmax(jnp.max(cell_rate), ('wide', 'narrow'))  41.1 us
    psum x1, blocking collectives, local(): summed = lax.psum(partial_value, ('wide', 'narrow'))  40 us
    dot_general x5, matrix products, block_product(): jnp.einsum('rkij,rkj->ri', matrix, picked, preferred_element_type=jnp.flo...  26 us
    ppermute x7, waiting for transfers between devices, _spread_frame(): oldest = jax.lax.ppermute(oldest, group_axis, passed)  23.4 us
    ppermute x16, waiting for transfers between devices, from_behind(): lax.ppermute(value, axis, [(source, source + steps) for source in range(l...  9.34 us
    unnamed x49, local copies, waits for them, and re-layouts  5.52 us
  transfers between devices with their start and end apart: 24, of which 10 were waited for; matrix products, arithmetic and copies ran while one was open for 22% of the time, Pallas kernels for 0%

profile of v1, /device:TPU:0, one launch (start us, length us, event | category | flops | bytes accessed | tf_op | source)
XLA Modules:
  0.0 231.0 jit_solution(11026153504620166475)
XLA Ops:
  10.3 4.9 %collective-permute-start = (bf16[8,128]{1,0:T(8,128)(2,1)S(1)}, bf16[8,128]{1,0:T(8,128)(2,1)S(1)}, u32[]{:S(2)}, u32[]{:S(2)}) collective-permute-start(bf16[8,128]{1,0:T(8,128)(2,1)S(1)} %get-tuple-element.29), channel_id=1, source_target_pairs={{0,8},{4,12},{8,16},{12,20},{16,24},{20,28},{1,9},{5,13},{9,17},{1... | collective-permute-start | bytes 6152 | tf_op jit(solution)/shard_map/ppermute | solution.py:28
  15.2 3.4 %collective-permute-start.1 = (bf16[8,128]{1,0:T(8,128)(2,1)S(1)}, bf16[8,128]{1,0:T(8,128)(2,1)S(1)}, u32[]{:S(2)}, u32[]{:S(2)}) collective-permute-start(bf16[8,128]{1,0:T(8,128)(2,1)S(1)} %get-tuple-element.28), channel_id=1, source_target_pairs={{0,4},{4,8},{8,12},{12,16},{16,20},{20,24},{24,28},{1,5},{5,9},{9,... | collective-permute-start | bytes 6152 | tf_op jit(solution)/shard_map/ppermute | solution.py:28
  23.5 3.2 %slice.70 = bf16[64,1,128,128]{3,2,1,0:T(8,128)(2,1)} slice(bf16[64,4,128,128]{3,2,1,0:T(8,128)(2,1)} %param.23), slice={[0:64], [0:1], [0:128], [0:128]} | slice | bytes 4194304 | tf_op jit(solution)/shard_map/slice | solution.py:94
  26.7 5.3 %copy.34 = bf16[64,1,128,128]{0,3,2,1:T(8,128)(2,1)} copy(bf16[64,1,128,128]{3,2,1,0:T(8,128)(2,1)} %slice.70) | data formatting | bytes 4194304
  35.2 5.7 %fusion.8 = f32[64,1,128,1]{2,1,3,0:T(1,128)S(1)} fusion(bf16[64,4,128,128]{3,2,1,0:T(8,128)(2,1)} %param.23, bf16[64,4,128,1]{2,1,0,3:T(4,128)(2,1)S(1)} %bitcast.130), kind=kOutput, calls=%fused_computation.22 | convolution fusion | flops 8388608 | bytes 8486912 | tf_op jit(solution)/shard_map/rkij,rkj->ri/dot_general | solution.py:33
  42.4 3.4 %fusion = f32[32,1,128,1]{2,1,3,0:T(1,128)S(1)} fusion(bf16[64,4,128,128]{3,2,1,0:T(8,128)(2,1)} %param.23, bf16[32,4,128,1]{2,1,0,3:T(4,128)(2,1)S(1)} %bitcast.137), kind=kOutput, calls=%fused_computation.14 | convolution fusion | flops 4194304 | bytes 4243456 | tf_op jit(solution)/shard_map/rkij,rkj->ri/dot_general | solution.py:33
  46.5 6.3 %collective-permute-start.4 = (bf16[8,128]{1,0:T(8,128)(2,1)S(1)}, bf16[8,128]{1,0:T(8,128)(2,1)S(1)}, u32[]{:S(2)}, u32[]{:S(2)}) collective-permute-start(bf16[8,128]{1,0:T(8,128)(2,1)S(1)} %get-tuple-element.25), channel_id=1, source_target_pairs={{0,8},{4,12},{8,16},{12,20},{16,24},{20,28},{1,9},{5,13},{9,17},{1... | collective-permute-start | bytes 6152 | tf_op jit(solution)/shard_map/ppermute | solution.py:28
  53.5 2.0 scatter_custom_fusion
  55.4 40.0 %psum.7 = f32[4096]{0:T(1024)S(1)} all-reduce(f32[4096]{0:T(1024)S(1)} %scatter_custom_fusion), channel_id=1, replica_groups=mesh['wide'=8,'narrow'=4] {'wide','narrow'}, use_global_device_ids=true, to_apply=%region_1.2 | all-reduce | flops 4096 | bytes 32768 | tf_op jit(solution)/shard_map/psum | solution.py:104
  95.4 4.2 %collective-permute-start.5 = (bf16[8,128]{1,0:T(8,128)(2,1)S(1)}, bf16[8,128]{1,0:T(8,128)(2,1)S(1)}, u32[]{:S(2)}, u32[]{:S(2)}) collective-permute-start(bf16[8,128]{1,0:T(8,128)(2,1)S(1)} %get-tuple-element.24), channel_id=1, source_target_pairs={{0,4},{4,8},{8,12},{12,16},{16,20},{20,24},{24,28},{1,5},{5,9},{9,... | collective-permute-start | bytes 6152 | tf_op jit(solution)/shard_map/ppermute | solution.py:28
  102.3 2.8 %collective-permute-done.6 = bf16[8,128]{1,0:T(8,128)(2,1)S(1)} collective-permute-done((bf16[8,128]{1,0:T(8,128)(2,1)S(1)}, bf16[8,128]{1,0:T(8,128)(2,1)S(1)}, u32[]{:S(2)}, u32[]{:S(2)}) %collective-permute-start.6) | collective-permute-done | bytes 2080 | tf_op jit(solution)/shard_map/ppermute | solution.py:28
  105.1 2.2 fusion.24
  108.2 5.4 %collective-permute-done.8 = f32[512]{0:T(512)S(1)} collective-permute-done((f32[512]{0:T(512)S(1)}, f32[512]{0:T(512)S(1)}, u32[]{:S(2)}, u32[]{:S(2)}) %collective-permute-start.8) | collective-permute-done | bytes 2080 | tf_op jit(solution)/shard_map/ppermute | solution.py:17
  114.5 5.4 %collective-permute-done.9 = f32[512]{0:T(512)S(1)} collective-permute-done((f32[512]{0:T(512)S(1)}, f32[512]{0:T(512)S(1)}, u32[]{:S(2)}, u32[]{:S(2)}) %collective-permute-start.9) | collective-permute-done | bytes 2080 | tf_op jit(solution)/shard_map/ppermute | solution.py:17
  119.9 5.6 %fusion.6 = f32[64,1,128,1]{2,1,3,0:T(1,128)S(1)} fusion(bf16[64,4,128,128]{3,2,1,0:T(8,128)(2,1)} %param.23, bf16[64,4,128,1]{2,1,0,3:T(4,128)(2,1)S(1)} %bitcast.128), kind=kOutput, calls=%fused_computation.20 | convolution fusion | flops 8388608 | bytes 8486912 | tf_op jit(solution)/shard_map/rkij,rkj->ri/dot_general | solution.py:33
  127.0 5.4 %collective-permute-done.11 = f32[512]{0:T(512)S(1)} collective-permute-done((f32[512]{0:T(512)S(1)}, f32[512]{0:T(512)S(1)}, u32[]{:S(2)}, u32[]{:S(2)}) %collective-permute-start.11) | collective-permute-done | bytes 2080 | tf_op jit(solution)/shard_map/ppermute | solution.py:17
  132.4 5.7 %fusion.4 = f32[64,1,128,1]{2,1,3,0:T(1,128)S(1)} fusion(bf16[64,4,128,128]{3,2,1,0:T(8,128)(2,1)} %param.23, bf16[64,4,128,1]{2,1,0,3:T(4,128)(2,1)S(1)} %bitcast.129), kind=kOutput, calls=%fused_computation.18 | convolution fusion | flops 8388608 | bytes 8486912 | tf_op jit(solution)/shard_map/rkij,rkj->ri/dot_general | solution.py:33
  139.6 5.4 %collective-permute-done.13 = f32[512]{0:T(512)S(1)} collective-permute-done((f32[512]{0:T(512)S(1)}, f32[512]{0:T(512)S(1)}, u32[]{:S(2)}, u32[]{:S(2)}) %collective-permute-start.13) | collective-permute-done | bytes 2080 | tf_op jit(solution)/shard_map/ppermute | solution.py:17
  145.0 5.6 %fusion.2 = f32[64,1,128,1]{2,1,3,0:T(1,128)S(1)} fusion(bf16[64,4,128,128]{3,2,1,0:T(8,128)(2,1)} %param.23, bf16[64,4,128,1]{2,1,0,3:T(4,128)(2,1)S(1)} %bitcast.127), kind=kOutput, calls=%fused_computation.16 | convolution fusion | flops 8388608 | bytes 8486912 | tf_op jit(solution)/shard_map/rkij,rkj->ri/dot_general | solution.py:33
  159.8 6.4 %collective-permute-start.19 = (f32[8,128]{1,0:T(8,128)S(1)}, f32[8,128]{1,0:T(8,128)S(1)}, u32[]{:S(2)}, u32[]{:S(2)}) collective-permute-start(f32[8,128]{1,0:T(8,128)S(1)} %get-tuple-element.17), channel_id=1, source_target_pairs={{0,8},{4,12},{8,16},{12,20},{16,24},{20,28},{1,9},{5,13},{9,17},{1... | collective-permute-start | bytes 12296 | tf_op jit(solution)/shard_map/ppermute | solution.py:28
  166.2 4.2 %collective-permute-start.20 = (f32[8,128]{1,0:T(8,128)S(1)}, f32[8,128]{1,0:T(8,128)S(1)}, u32[]{:S(2)}, u32[]{:S(2)}) collective-permute-start(f32[8,128]{1,0:T(8,128)S(1)} %get-tuple-element.16), channel_id=1, source_target_pairs={{0,4},{4,8},{8,12},{12,16},{16,20},{20,24},{24,28},{1,5},{5,9},{9,... | collective-permute-start | bytes 12296 | tf_op jit(solution)/shard_map/ppermute | solution.py:28
  173.1 3.8 %collective-permute-done.21 = f32[8,128]{1,0:T(8,128)S(1)} collective-permute-done((f32[8,128]{1,0:T(8,128)S(1)}, f32[8,128]{1,0:T(8,128)S(1)}, u32[]{:S(2)}, u32[]{:S(2)}) %collective-permute-start.21) | collective-permute-done | bytes 4128 | tf_op jit(solution)/shard_map/ppermute | solution.py:28
  177.6 2.7 %collective-permute-done.22 = f32[8,128]{1,0:T(8,128)S(1)} collective-permute-done((f32[8,128]{1,0:T(8,128)S(1)}, f32[8,128]{1,0:T(8,128)S(1)}, u32[]{:S(2)}, u32[]{:S(2)}) %collective-permute-start.22) | collective-permute-done | bytes 4128 | tf_op jit(solution)/shard_map/ppermute | solution.py:28
  181.8 41.1 %pmax.7 = f32[]{:T(128)} all-reduce(f32[]{:T(128)} %fusion.16), channel_id=1, replica_groups=mesh['wide'=8,'narrow'=4] {'wide','narrow'}, use_global_device_ids=true, to_apply=%region_4.5 | all-reduce | flops 1 | bytes 8 | tf_op jit(solution)/shard_map/pmax | solution.py:133
  (149 shorter events, 35.7 us)
Async XLA Ops:
  7.2 97.9 %all-gather.2.cloned.1.call-start = ((), (), s32[]{:S(2)}) async-start(), calls=%async_computation | async-start | bytes 1310720 | tf_op jit(solution)/shard_map/all_gather | solution.py:108
  10.3 31.3 %collective-permute-start = (bf16[8,128]{1,0:T(8,128)(2,1)S(1)}, bf16[8,128]{1,0:T(8,128)(2,1)S(1)}, u32[]{:S(2)}, u32[]{:S(2)}) collective-permute-start(bf16[8,128]{1,0:T(8,128)(2,1)S(1)} %get-tuple-element.29), channel_id=1, source_target_pairs={{0,8},{4,12},{8,16},{12,20},{16,24},{20,28},{1,9},{5,13},{9,17},{1... | collective-permute-start | bytes 6152 | tf_op jit(solution)/shard_map/ppermute | solution.py:28
  15.2 26.4 %collective-permute-start.1 = (bf16[8,128]{1,0:T(8,128)(2,1)S(1)}, bf16[8,128]{1,0:T(8,128)(2,1)S(1)}, u32[]{:S(2)}, u32[]{:S(2)}) collective-permute-start(bf16[8,128]{1,0:T(8,128)(2,1)S(1)} %get-tuple-element.28), channel_id=1, source_target_pairs={{0,4},{4,8},{8,12},{12,16},{16,20},{20,24},{24,28},{1,5},{5,9},{9,... | collective-permute-start | bytes 6152 | tf_op jit(solution)/shard_map/ppermute | solution.py:28
  18.6 23.0 %collective-permute-start.2 = (bf16[8,128]{1,0:T(8,128)(2,1)S(1)}, bf16[8,128]{1,0:T(8,128)(2,1)S(1)}, u32[]{:S(2)}, u32[]{:S(2)}) collective-permute-start(bf16[8,128]{1,0:T(8,128)(2,1)S(1)} %get-tuple-element.27), channel_id=1, source_target_pairs={{4,0},{8,4},{12,8},{16,12},{20,16},{24,20},{28,24},{5,1},{9,5},{13... | collective-permute-start | bytes 6152 | tf_op jit(solution)/shard_map/ppermute | solution.py:28
  19.9 21.8 %collective-permute-start.3 = (bf16[8,128]{1,0:T(8,128)(2,1)S(1)}, bf16[8,128]{1,0:T(8,128)(2,1)S(1)}, u32[]{:S(2)}, u32[]{:S(2)}) collective-permute-start(bf16[8,128]{1,0:T(8,128)(2,1)S(1)} %get-tuple-element.26), channel_id=1, source_target_pairs={{8,0},{12,4},{16,8},{20,12},{24,16},{28,20},{9,1},{13,5},{17,9},{2... | collective-permute-start | bytes 6152 | tf_op jit(solution)/shard_map/ppermute | solution.py:28
  46.5 55.8 %collective-permute-start.4 = (bf16[8,128]{1,0:T(8,128)(2,1)S(1)}, bf16[8,128]{1,0:T(8,128)(2,1)S(1)}, u32[]{:S(2)}, u32[]{:S(2)}) collective-permute-start(bf16[8,128]{1,0:T(8,128)(2,1)S(1)} %get-tuple-element.25), channel_id=1, source_target_pairs={{0,8},{4,12},{8,16},{12,20},{16,24},{20,28},{1,9},{5,13},{9,17},{1... | collective-permute-start | bytes 6152 | tf_op jit(solution)/shard_map/ppermute | solution.py:28
  95.4 6.9 %collective-permute-start.5 = (bf16[8,128]{1,0:T(8,128)(2,1)S(1)}, bf16[8,128]{1,0:T(8,128)(2,1)S(1)}, u32[]{:S(2)}, u32[]{:S(2)}) collective-permute-start(bf16[8,128]{1,0:T(8,128)(2,1)S(1)} %get-tuple-element.24), channel_id=1, source_target_pairs={{0,4},{4,8},{8,12},{12,16},{16,20},{20,24},{24,28},{1,5},{5,9},{9,... | collective-permute-start | bytes 6152 | tf_op jit(solution)/shard_map/ppermute | solution.py:28
  99.6 5.5 %collective-permute-start.6 = (bf16[8,128]{1,0:T(8,128)(2,1)S(1)}, bf16[8,128]{1,0:T(8,128)(2,1)S(1)}, u32[]{:S(2)}, u32[]{:S(2)}) collective-permute-start(bf16[8,128]{1,0:T(8,128)(2,1)S(1)} %get-tuple-element.23), channel_id=1, source_target_pairs={{4,0},{8,4},{12,8},{16,12},{20,16},{24,20},{28,24},{5,1},{9,5},{13... | collective-permute-start | bytes 6152 | tf_op jit(solution)/shard_map/ppermute | solution.py:28
  100.9 7.3 %collective-permute-start.7 = (bf16[8,128]{1,0:T(8,128)(2,1)S(1)}, bf16[8,128]{1,0:T(8,128)(2,1)S(1)}, u32[]{:S(2)}, u32[]{:S(2)}) collective-permute-start(bf16[8,128]{1,0:T(8,128)(2,1)S(1)} %get-tuple-element.22), channel_id=1, source_target_pairs={{8,0},{12,4},{16,8},{20,12},{24,16},{28,20},{9,1},{13,5},{17,9},{2... | collective-permute-start | bytes 6152 | tf_op jit(solution)/shard_map/ppermute | solution.py:28
  107.3 6.3 %collective-permute-start.8 = (f32[512]{0:T(512)S(1)}, f32[512]{0:T(512)S(1)}, u32[]{:S(2)}, u32[]{:S(2)}) collective-permute-start(f32[512]{0:T(512)S(1)} %bitcast.138), channel_id=1, source_target_pairs={{0,4},{4,8},{8,12},{12,16},{16,20},{20,24},{24,28},{28,0},{1,5},{5... | collective-permute-start | bytes 6152 | tf_op jit(solution)/shard_map/ppermute | solution.py:17
  113.6 6.3 %collective-permute-start.9 = (f32[512]{0:T(512)S(1)}, f32[512]{0:T(512)S(1)}, u32[]{:S(2)}, u32[]{:S(2)}) collective-permute-start(f32[512]{0:T(512)S(1)} %collective-permute-done.8), channel_id=1, source_target_pairs={{0,4},{4,8},{8,12},{12,16},{16,20},{20,24},{24,28},{28,0},{1,5},{5... | collective-permute-start | bytes 6152 | tf_op jit(solution)/shard_map/ppermute | solution.py:17
  119.9 6.3 %collective-permute-start.10 = (f32[512]{0:T(512)S(1)}, f32[512]{0:T(512)S(1)}, u32[]{:S(2)}, u32[]{:S(2)}) collective-permute-start(f32[512]{0:T(512)S(1)} %collective-permute-done.9), channel_id=1, source_target_pairs={{0,4},{4,8},{8,12},{12,16},{16,20},{20,24},{24,28},{28,0},{1,5},{5... | collective-permute-start | bytes 6152 | tf_op jit(solution)/shard_map/ppermute | solution.py:17
  126.1 6.3 %collective-permute-start.11 = (f32[512]{0:T(512)S(1)}, f32[512]{0:T(512)S(1)}, u32[]{:S(2)}, u32[]{:S(2)}) collective-permute-start(f32[512]{0:T(512)S(1)} %collective-permute-done.10), channel_id=1, source_target_pairs={{0,4},{4,8},{8,12},{12,16},{16,20},{20,24},{24,28},{28,0},{1,5},{5... | collective-permute-start | bytes 6152 | tf_op jit(solution)/shard_map/ppermute | solution.py:17
  132.4 6.3 %collective-permute-start.12 = (f32[512]{0:T(512)S(1)}, f32[512]{0:T(512)S(1)}, u32[]{:S(2)}, u32[]{:S(2)}) collective-permute-start(f32[512]{0:T(512)S(1)} %collective-permute-done.11), channel_id=1, source_target_pairs={{0,4},{4,8},{8,12},{12,16},{16,20},{20,24},{24,28},{28,0},{1,5},{5... | collective-permute-start | bytes 6152 | tf_op jit(solution)/shard_map/ppermute | solution.py:17
  138.7 6.3 %collective-permute-start.13 = (f32[512]{0:T(512)S(1)}, f32[512]{0:T(512)S(1)}, u32[]{:S(2)}, u32[]{:S(2)}) collective-permute-start(f32[512]{0:T(512)S(1)} %collective-permute-done.12), channel_id=1, source_target_pairs={{0,4},{4,8},{8,12},{12,16},{16,20},{20,24},{24,28},{28,0},{1,5},{5... | collective-permute-start | bytes 6152 | tf_op jit(solution)/shard_map/ppermute | solution.py:17
  145.0 6.3 %collective-permute-start.14 = (f32[512]{0:T(512)S(1)}, f32[512]{0:T(512)S(1)}, u32[]{:S(2)}, u32[]{:S(2)}) collective-permute-start(f32[512]{0:T(512)S(1)} %collective-permute-done.13), channel_id=1, source_target_pairs={{0,4},{4,8},{8,12},{12,16},{16,20},{20,24},{24,28},{28,0},{1,5},{5... | collective-permute-start | bytes 6152 | tf_op jit(solution)/shard_map/ppermute | solution.py:17
  154.6 11.6 %collective-permute-start.15 = (f32[8,128]{1,0:T(8,128)S(1)}, f32[8,128]{1,0:T(8,128)S(1)}, u32[]{:S(2)}, u32[]{:S(2)}) collective-permute-start(f32[8,128]{1,0:T(8,128)S(1)} %get-tuple-element.21), channel_id=1, source_target_pairs={{0,8},{4,12},{8,16},{12,20},{16,24},{20,28},{1,9},{5,13},{9,17},{1... | collective-permute-start | bytes 12296 | tf_op jit(solution)/shard_map/ppermute | solution.py:28
  155.9 14.5 %collective-permute-start.16 = (f32[8,128]{1,0:T(8,128)S(1)}, f32[8,128]{1,0:T(8,128)S(1)}, u32[]{:S(2)}, u32[]{:S(2)}) collective-permute-start(f32[8,128]{1,0:T(8,128)S(1)} %get-tuple-element.20), channel_id=1, source_target_pairs={{0,4},{4,8},{8,12},{12,16},{16,20},{20,24},{24,28},{1,5},{5,9},{9,... | collective-permute-start | bytes 12296 | tf_op jit(solution)/shard_map/ppermute | solution.py:28
  157.2 14.5 %collective-permute-start.17 = (f32[8,128]{1,0:T(8,128)S(1)}, f32[8,128]{1,0:T(8,128)S(1)}, u32[]{:S(2)}, u32[]{:S(2)}) collective-permute-start(f32[8,128]{1,0:T(8,128)S(1)} %get-tuple-element.19), channel_id=1, source_target_pairs={{4,0},{8,4},{12,8},{16,12},{20,16},{24,20},{28,24},{5,1},{9,5},{13... | collective-permute-start | bytes 12296 | tf_op jit(solution)/shard_map/ppermute | solution.py:28
  158.5 14.5 %collective-permute-start.18 = (f32[8,128]{1,0:T(8,128)S(1)}, f32[8,128]{1,0:T(8,128)S(1)}, u32[]{:S(2)}, u32[]{:S(2)}) collective-permute-start(f32[8,128]{1,0:T(8,128)S(1)} %get-tuple-element.18), channel_id=1, source_target_pairs={{8,0},{12,4},{16,8},{20,12},{24,16},{28,20},{9,1},{13,5},{17,9},{2... | collective-permute-start | bytes 12296 | tf_op jit(solution)/shard_map/ppermute | solution.py:28
  159.8 13.2 %collective-permute-start.19 = (f32[8,128]{1,0:T(8,128)S(1)}, f32[8,128]{1,0:T(8,128)S(1)}, u32[]{:S(2)}, u32[]{:S(2)}) collective-permute-start(f32[8,128]{1,0:T(8,128)S(1)} %get-tuple-element.17), channel_id=1, source_target_pairs={{0,8},{4,12},{8,16},{12,20},{16,24},{20,28},{1,9},{5,13},{9,17},{1... | collective-permute-start | bytes 12296 | tf_op jit(solution)/shard_map/ppermute | solution.py:28
  166.2 6.9 %collective-permute-start.20 = (f32[8,128]{1,0:T(8,128)S(1)}, f32[8,128]{1,0:T(8,128)S(1)}, u32[]{:S(2)}, u32[]{:S(2)}) collective-permute-start(f32[8,128]{1,0:T(8,128)S(1)} %get-tuple-element.16), channel_id=1, source_target_pairs={{0,4},{4,8},{8,12},{12,16},{16,20},{20,24},{24,28},{1,5},{5,9},{9,... | collective-permute-start | bytes 12296 | tf_op jit(solution)/shard_map/ppermute | solution.py:28
  170.4 6.5 %collective-permute-start.21 = (f32[8,128]{1,0:T(8,128)S(1)}, f32[8,128]{1,0:T(8,128)S(1)}, u32[]{:S(2)}, u32[]{:S(2)}) collective-permute-start(f32[8,128]{1,0:T(8,128)S(1)} %get-tuple-element.15), channel_id=1, source_target_pairs={{4,0},{8,4},{12,8},{16,12},{20,16},{24,20},{28,24},{5,1},{9,5},{13... | collective-permute-start | bytes 12296 | tf_op jit(solution)/shard_map/ppermute | solution.py:28
  171.7 8.6 %collective-permute-start.22 = (f32[8,128]{1,0:T(8,128)S(1)}, f32[8,128]{1,0:T(8,128)S(1)}, u32[]{:S(2)}, u32[]{:S(2)}) collective-permute-start(f32[8,128]{1,0:T(8,128)S(1)} %get-tuple-element.14), channel_id=1, source_target_pairs={{8,0},{12,4},{16,8},{20,12},{24,16},{28,20},{9,1},{13,5},{17,9},{2... | collective-permute-start | bytes 12296 | tf_op jit(solution)/shard_map/ppermute | solution.py:28
  (10 other events, 394.0 us)
Sparse Core Ops, SparseCore 0:
  21.3 20.1 all-gather.1
